TPU v7x, 256 devices: a whole 4x4x8 slice. The times are simulated.
256 devices in a mesh: frame: 4 (over x), space: 64 (over z, y, core).
Axes of the slice: x: 4, y: 4, z: 8, core: 2. Of those that a mesh axis runs over, the one named last changes fastest.
Arguments:
- queries: bfloat16 [32768, 3072], P(('frame', 'space')), as said below
- keys: bfloat16 [32768, 3072], P(('frame', 'space')), as said below
- values: bfloat16 [32768, 3072], P(('frame', 'space')), may hold values from -5 to 5
- level_weight: float32 [3, 24, 32768], P(None, None, ('frame', 'space')), may hold values from 0.2 to 2
- frame_len: int32 [256, 4], P(('frame', 'space')), may hold values from 1 to 53, 128 in all within a row
- window_back: int32 [256, 4], P(('frame', 'space')), may hold values from 2 to 63
Outputs:
- mixed: bfloat16 [32768, 3072], P(('frame', 'space'))
Inputs may be any that keep to these rules, and one draw needn't show every extreme that they name: `queries`: entries up to 60 in magnitude. `keys`: entries up to 4 in magnitude. `frame_len`: each row is the frame lengths of one device's 128 tokens, summing to 128; the longest frame of each row has exactly 53 tokens.
All inputs are finite; a program needn't handle non-finite values.
Results may differ from a plain program's by a relative error of at most 0.0085.
Values may be sent and summed in bfloat16 or wider, within the bound.
A program may use at most 64 MiB of HBM per device.

v0:
```python
import math
import jax
import jax.numpy as jnp
from jax import lax
from jax.sharding import PartitionSpec as P

HEADS = 24
HEAD_DIM = 128
EPSILON = 1e-06


def unit_rows(matrix):
    return (matrix * lax.rsqrt(jnp.mean(matrix * matrix, -1, keepdims=True) + EPSILON)).astype(
        jnp.bfloat16
    )


def visible_mask(lengths, backward, count):
    starts = jnp.cumsum(lengths) - lengths
    lowest = jnp.maximum(starts - backward, 0)
    position = jnp.arange(count, dtype=jnp.int32)
    inside = (position[:, None] >= starts[None, :]).astype(jnp.int32)
    frame_of = jnp.sum(inside, 1) - 1
    onehot = frame_of[:, None] == jnp.arange(lengths.shape[0], dtype=jnp.int32)[None, :]
    floor_row = jnp.sum(jnp.where(onehot, lowest[None, :], 0), 1)
    return (position[None, :] <= position[:, None]) & (position[None, :] >= floor_row[:, None])


def causal_mix(query_heads, key_heads, value_heads, visible, heads, head_dim):
    pieces = []
    for first_head in range(0, heads, 4):
        query_part = query_heads[:, first_head : first_head + 4]
        key_part = key_heads[:, first_head : first_head + 4]
        value_part = value_heads[:, first_head : first_head + 4]
        scores = jnp.einsum(
            "thd,shd->hts", query_part, key_part, preferred_element_type=jnp.float32
        ) / math.sqrt(head_dim)
        scores = jnp.where(visible[None], scores, -jnp.inf)
        row_max = jnp.max(scores, -1, keepdims=True)
        weights = jnp.exp(scores - row_max)
        totals = jnp.sum(weights, -1)
        mixed_part = jnp.einsum(
            "hts,shd->thd",
            weights.astype(jnp.bfloat16),
            value_part,
            preferred_element_type=jnp.float32,
        )
        pieces.append(mixed_part / jnp.transpose(totals)[:, :, None])
    return jnp.concatenate(pieces, 1)


def body(queries, keys, values, level_weight, frame_len, window_back):
    tok_rows = queries.shape[0]
    frames_total = lax.axis_size("frame")
    frame_pos = lax.axis_index("frame")
    space_count = lax.axis_size("space")
    query_heads = queries.reshape(tok_rows, HEADS, HEAD_DIM)
    key_heads = keys.reshape(tok_rows, HEADS, HEAD_DIM)
    value_heads = values.reshape(tok_rows, HEADS, HEAD_DIM)
    normal_k = unit_rows(key_heads.astype(jnp.float32))
    local_state = jnp.einsum(
        "thd,the->hde", normal_k, value_heads, preferred_element_type=jnp.float32
    )
    state_rows = local_state.reshape(HEADS * HEAD_DIM, HEAD_DIM)
    block_part = lax.psum(state_rows, "space")
    tree_depth = frames_total.bit_length() - 1
    levels = []
    all_blocks = lax.all_gather(
        block_part[None].astype(jnp.bfloat16), "frame", axis=0, tiled=True
    ).astype(jnp.float32)
    block_ids = jnp.arange(frames_total, dtype=jnp.int32)
    for bit_index in range(tree_depth):
        start_block = frame_pos // 2 ** (bit_index + 1) * 2 ** (bit_index + 1)
        bit_set = frame_pos // 2**bit_index % 2
        inside = (
            (block_ids >= start_block) & (block_ids < start_block + 2**bit_index) & (bit_set == 1)
        )
        levels.append(jnp.sum(jnp.where(inside[:, None, None], all_blocks, 0.0), 0))
    level_rows = jnp.stack(levels).astype(jnp.bfloat16)
    level_heads = level_rows.reshape(tree_depth, HEADS, HEAD_DIM, HEAD_DIM)
    visible = visible_mask(frame_len[0], window_back[0], tok_rows)
    local_mix = causal_mix(query_heads, key_heads, value_heads, visible, HEADS, HEAD_DIM)
    result = local_mix * jnp.transpose(level_weight[0])[:, :, None]
    normal_q = unit_rows(query_heads.astype(jnp.float32))
    level_reads = jnp.einsum(
        "thd,lhde->lthe", normal_q, level_heads, preferred_element_type=jnp.float32
    )
    block_tokens = tok_rows * space_count
    for level_index in range(tree_depth):
        level_scale = 1.0 / math.sqrt(HEAD_DIM * 2**level_index * block_tokens)
        result = result + jnp.transpose(level_weight[1 + level_index])[:, :, None] * (
            level_scale * level_reads[level_index]
        )
    return result.reshape(tok_rows, HEADS * HEAD_DIM).astype(jnp.bfloat16)


def solution(mesh):
    return jax.shard_map(
        body,
        mesh=mesh,
        in_specs=(
            P(("frame", "space"), None),
            P(("frame", "space"), None),
            P(("frame", "space"), None),
            P(None, None, ("frame", "space")),
            P(("frame", "space"), None),
            P(("frame", "space"), None),
        ),
        out_specs=P(("frame", "space"), None),
        check_vma=False,
    )
```

profile of v0, /device:TPU:1, one launch (start us, length us, event | category | flops | bytes accessed | tf_op | source)
XLA Modules:
  0.0 333.2 jit_solution(7249709284273984305)
XLA Ops:
  6.5 1.6 copy.53
  8.1 0.4 copy.55
  8.7 0.7 fusion.32
  9.4 264.9 %all-reduce.1 = bf16[3072,128]{1,0:T(8,128)(2,1)} all-reduce(f32[3072,128]{1,0:T(8,128)S(1)} %bitcast.114), channel_id=1, replica_groups=mesh['frame'=4,'space'=64] {'space'}, use_global_device_ids=true, to_apply=%region_16.17 | all-reduce | flops 393216 | bytes 2359296 | tf_op jit(solution)/shard_map/psum | solution.py:65
  274.8 1.2 copy.51
  276.0 1.2 fusion.75
  277.3 1.2 fusion.76
  278.6 1.2 fusion.77
  279.9 1.2 fusion.78
  281.2 1.2 fusion.79
  282.5 1.2 fusion.80
  285.1 1.6 copy.78
  287.1 29.0 %all-gather.3.cloned.1.call-done = bf16[12288,128]{1,0:T(8,128)(2,1)} async-done(((bf16[3072,128]{1,0:T(8,128)(2,1)}), bf16[12288,128]{1,0:T(8,128)(2,1)}) %all-gather.3.cloned.1.call-update) | async-done | bytes 3145744 | tf_op jit(solution)/shard_map/all_gather | solution.py:68
  316.1 3.1 fusion
  319.2 0.4 copy.73
  319.6 0.4 copy.74
  320.0 0.6 convolution_bitcast_fusion
  320.7 1.6 copy.77
  322.4 0.5 copy.80
  322.9 0.5 mul.97
  323.3 0.5 mul.104
  323.8 0.4 copy-done.2
  324.3 0.5 copy-done.3
  324.7 1.6 fusion.7
  (46 shorter events, 2.8 us)
Async XLA Ops:
  6.5 1.6 copy-start.4
  6.5 309.5 %all-gather.3.cloned.1.call-start = ((), (), s32[]{:S(2)}) async-start(), calls=%async_computation | async-start | bytes 3932160 | tf_op jit(solution)/shard_map/all_gather | solution.py:68
  8.1 1.3 copy-start.1
  9.4 265.0 %copy-start.7 = (s32[1,4]{1,0:T(1,128)S(1)}, s32[1,4]{1,0:T(1,128)}, u32[]{:S(2)}) copy-start(s32[1,4]{1,0:T(1,128)} %param.10) | copy-start | bytes 52
  9.4 265.2 %copy-start.8 = (s32[1,4]{1,0:T(1,128)S(1)}, s32[1,4]{1,0:T(1,128)}, u32[]{:S(2)}) copy-start(s32[1,4]{1,0:T(1,128)} %param.11) | copy-start | bytes 52
  9.4 265.4 %copy-start.5 = (bf16[128,3072]{1,0:T(8,128)(2,1)S(1)}, bf16[128,3072]{1,0:T(8,128)(2,1)}, u32[]{:S(2)}) copy-start(bf16[128,3072]{1,0:T(8,128)(2,1)} %param.6) | copy-start | bytes 2359300
  279.9 3.9 %copy-start.6 = (f32[3,24,128]{2,1,0:T(8,128)S(1)}, f32[3,24,128]{2,1,0:T(8,128)}, u32[]{:S(2)}) copy-start(f32[3,24,128]{2,1,0:T(8,128)} %param.9) | copy-start | bytes 110596
  285.1 1.8 copy-start
  322.8 1.4 copy-start.2
  322.9 1.9 copy-start.3
Sparse Core Ops, SparseCore 0:
  274.5 41.5 all-gather.2
where the time goes:
time: 333 us
  blocking collectives  265 us (80%)
  waiting for transfers between devices  29 us (9%)
  between operations  13.7 us (4%)
  local copies, waits for them, and re-layouts  9.88 us (3%)
  matrix products  9.67 us (3%)
  other arithmetic  6 us (2%)
    psum x1, blocking collectives, body(): block_part = lax.psum(state_rows, 'space')  265 us
    all_gather x1, waiting for transfers between devices, body(): lax.all_gather(block_part[None].astype(jnp.bfloat16), 'frame', axis=0, ti...  29 us
    dot_general x6, matrix products, causal_mix(): jnp.einsum('thd,shd->hts', query_part, key_part, preferred_element_type=j...  7.32 us
  transfers between devices with their start and end apart: 1, of which 1 were waited for; matrix products, arithmetic and copies ran while one was open for 4% of the time, Pallas kernels for 0%

commit v1 on v0

--- a/solution.py
+++ b/solution.py
@@ -7,6 +7,11 @@
 HEADS = 24
 HEAD_DIM = 128
 EPSILON = 1e-06
+
+
+def all_by_exchange(x, axis, d):
+    sent = jnp.stack([x] * lax.axis_size(axis))
+    return jnp.concatenate(lax.all_to_all(sent, axis, 0, 0), axis=d)
 
 
 def unit_rows(matrix):
@@ -65,9 +70,9 @@
     block_part = lax.psum(state_rows, "space")
     tree_depth = frames_total.bit_length() - 1
     levels = []
-    all_blocks = lax.all_gather(
-        block_part[None].astype(jnp.bfloat16), "frame", axis=0, tiled=True
-    ).astype(jnp.float32)
+    all_blocks = all_by_exchange(block_part[None].astype(jnp.bfloat16), "frame", 0).astype(
+        jnp.float32
+    )
     block_ids = jnp.arange(frames_total, dtype=jnp.int32)
     for bit_index in range(tree_depth):
         start_block = frame_pos // 2 ** (bit_index + 1) * 2 ** (bit_index + 1)

time: 333 us -> 321 us (0.964); the launches traced: 333 us -> 316 us
  waiting for transfers between devices: 29 us -> 8.85 us
  between operations: 13.7 us -> 0.37 us
  other arithmetic: 6 us -> 12.6 us
  local copies, waits for them, and re-layouts: 9.88 us -> 16.3 us
  starting transfers between devices: 0.01 us -> 4.01 us
    all_gather x1 -> x0, waiting for transfers between devices: 29 us -> none  [body(): lax.all_gather(block_part[None].astype(jnp.bfloat16), 'frame', axis=0, ti...]
    all_to_all x0 -> x1, waiting for transfers between devices: none -> 8.85 us  [all_by_exchange(): return jnp.concatenate(lax.all_to_all(sent, axis, 0, 0), axis=d)]
    reduce_sum x6, other arithmetic: 0.37 us -> 5.24 us  [causal_mix(): totals = jnp.sum(weights, -1)]
    all_to_all x0 -> x1, starting transfers between devices: none -> 4.01 us  [all_by_exchange(): return jnp.concatenate(lax.all_to_all(sent, axis, 0, 0), axis=d)]
  transfers between devices with their start and end apart: 1 -> 1, of which waited for: 1 -> 1; matrix products, arithmetic and copies ran while one was open for 4% -> 7% of each run, Pallas kernels for 0% -> 0%
where the time goes in v1:
time: 321 us; the launch traced here: 316 us
  blocking collectives  264 us (82%)
  local copies, waits for them, and re-layouts  16.3 us (5%)
  other arithmetic  12.6 us (4%)
  matrix products  9.34 us (3%)
  waiting for transfers between devices  8.85 us (3%)
  starting transfers between devices  4.01 us (1%)
    psum x1, blocking collectives, body(): block_part = lax.psum(state_rows, 'space')  264 us
    all_to_all x1, waiting for transfers between devices, all_by_exchange(): return jnp.concatenate(lax.all_to_all(sent, axis, 0, 0), axis=d)  8.85 us
    dot_general x6, matrix products, causal_mix(): jnp.einsum('thd,shd->hts', query_part, key_part, preferred_element_type=j...  7 us
  transfers between devices with their start and end apart: 1, of which 1 were waited for; matrix products, arithmetic and copies ran while one was open for 7% of the time, Pallas kernels for 0%

profile of v1, /device:TPU:1, one launch (start us, length us, event | category | flops | bytes accessed | tf_op | source)
XLA Modules:
  0.0 315.8 jit_solution(2419693226612850592)
XLA Ops:
  0.0 1.6 copy.83
  2.2 0.7 fusion.32
  2.9 264.3 %all-reduce.1 = bf16[3072,128]{1,0:T(8,128)(2,1)S(1)} all-reduce(f32[3072,128]{1,0:T(8,128)S(1)} %bitcast.116), channel_id=1, replica_groups=mesh['frame'=4,'space'=64] {'space'}, use_global_device_ids=true, to_apply=%region_16.17 | all-reduce | flops 393216 | bytes 2359296 | tf_op jit(solution)/shard_map/psum | solution.py:70
  267.1 2.1 stack.16
  269.2 4.0 %all-to-all-start = ((bf16[4,1,3072,128]{3,2,1,0:T(8,128)(2,1)}), bf16[4,1,3072,128]{3,2,1,0:T(8,128)(2,1)S(1)}, u32[]{:S(2)}, u32[]{:S(2)}) async-start(bf16[4,1,3072,128]{3,2,1,0:T(8,128)(2,1)} %stack.16), calls=%async_computation | async-start | bytes 6291456 | tf_op jit(solution)/shard_map/all_to_all | solution.py:14
  273.2 2.3 copy.81
  276.0 2.0 fusion.75
  278.0 1.9 fusion.76
  279.9 0.9 fusion.77
  280.8 0.9 fusion.78
  281.8 0.9 fusion.79
  283.1 1.1 fusion.36
  284.2 1.0 fusion.38
  285.2 1.0 fusion.40
  286.2 1.0 fusion.42
  287.2 1.1 fusion.44
  290.1 1.4 broadcast_multiply_fusion
  291.5 3.0 copy.108
  294.7 1.3 fusion.4
  296.0 8.8 %all-to-all-done = bf16[4,1,3072,128]{3,2,1,0:T(8,128)(2,1)S(1)} async-done(((bf16[4,1,3072,128]{3,2,1,0:T(8,128)(2,1)}), bf16[4,1,3072,128]{3,2,1,0:T(8,128)(2,1)S(1)}, u32[]{:S(2)}, u32[]{:S(2)}) %all-to-all-start) | async-done | bytes 3145760 | tf_op jit(solution)/shard_map/all_to_all | solution.py:14
  304.9 2.5 fusion
  307.4 1.6 copy.103
  310.2 1.6 copy.107
  314.2 1.6 fusion.7
  (64 shorter events, 6.7 us)
Async XLA Ops:
  0.0 1.6 copy-start.9
  1.6 1.3 copy-start.2
  2.0 0.9 copy-start.7
  269.2 35.6 %all-to-all-start = ((bf16[4,1,3072,128]{3,2,1,0:T(8,128)(2,1)}), bf16[4,1,3072,128]{3,2,1,0:T(8,128)(2,1)S(1)}, u32[]{:S(2)}, u32[]{:S(2)}) async-start(bf16[4,1,3072,128]{3,2,1,0:T(8,128)(2,1)} %stack.16), calls=%async_computation | async-start | bytes 6291456 | tf_op jit(solution)/shard_map/all_to_all | solution.py:14
  273.2 2.3 copy-start.16
  273.2 2.5 copy-start.17
  275.7 4.1 %copy-start = (bf16[128,3072]{0,1:T(8,128)(2,1)S(1)}, bf16[128,3072]{0,1:T(8,128)(2,1)}, u32[]{:S(2)}) copy-start(bf16[128,3072]{0,1:T(8,128)(2,1)} %copy.81) | copy-start | bytes 2359300
  275.7 4.1 %copy-start.3 = (bf16[128,3072]{0,1:T(8,128)(2,1)S(1)}, bf16[128,3072]{0,1:T(8,128)(2,1)}, u32[]{:S(2)}) copy-start(bf16[128,3072]{0,1:T(8,128)(2,1)} %copy-done.2) | copy-start | bytes 2359300
  279.9 3.1 copy-start.15
  283.0 5.3 %copy-start.8 = (bf16[128,3072]{0,1:T(8,128)(2,1)S(1)}, bf16[128,3072]{0,1:T(8,128)(2,1)}, u32[]{:S(2)}) copy-start(bf16[128,3072]{0,1:T(8,128)(2,1)} %copy-done.7) | copy-start | bytes 2359300
  283.0 5.3 %copy-start.14 = (f32[4,128,128]{1,2,0:T(8,128)S(1)}, f32[4,128,128]{1,2,0:T(8,128)}, u32[]{:S(2)}) copy-start(f32[4,128,128]{1,2,0:T(8,128)} %get-tuple-element.15) | copy-start | bytes 786436
  283.0 5.5 %copy-start.13 = (f32[4,128,128]{1,2,0:T(8,128)S(1)}, f32[4,128,128]{1,2,0:T(8,128)}, u32[]{:S(2)}) copy-start(f32[4,128,128]{1,2,0:T(8,128)} %get-tuple-element.17) | copy-start | bytes 786436
  287.2 1.6 copy-start.12
  288.5 1.0 copy-start.11
  288.7 1.0 copy-start.10
  307.4 1.6 copy-start.6
  307.4 2.0 copy-start.1
  312.3 1.4 copy-start.4
  312.3 1.9 copy-start.5
